TPU v7x, 512 devices: a whole 4x8x8 slice. The times are simulated.
512 devices in a mesh: dp: 16 (over z, core), ctx: 32 (over y, x).
Axes of the slice: x: 4, y: 8, z: 8, core: 2. Of those that a mesh axis runs over, the one named last changes fastest.
Arguments:
- query_in: bfloat16 [16, 8192, 1280], P('dp', 'ctx'), may hold values from -150 to 150
- key_in: bfloat16 [16, 8192, 1280], P('dp', 'ctx'), may hold values from -16 to 16
- value_in: bfloat16 [16, 8192, 1280], P('dp', 'ctx'), may hold values from -6 to 6
- grad_out: bfloat16 [16, 8192, 1280], P('dp', 'ctx'), may hold values from -6 to 6
- key_blocks: int32 [10, 32, 6], P(None, 'ctx'), may hold values from 0 to 63, as said below
- sink_logits: float32 [10], replicated, may hold values from 3 to 8
Outputs:
- grad_query: bfloat16 [16, 8192, 1280], P('dp', 'ctx')
- grad_key: bfloat16 [16, 8192, 1280], P('dp', 'ctx')
- grad_value: bfloat16 [16, 8192, 1280], P('dp', 'ctx')
- grad_sink: float32 [10], replicated
Inputs may be any that keep to these rules, and one draw needn't show every extreme that they name: `key_blocks`: block b holds tokens 128 b to 128 b + 127. The 6 entries of one head and segment are distinct, and none falls in the aligned group of 256 tokens that holds the segment. Counting all heads, entries and segments of one aligned group of 256 tokens, at most 2 entries fall in any one other aligned group of 256 tokens, and every group reaches 2 with some other group in every draw.
All inputs are finite; a program needn't handle non-finite values.
Results may differ from a plain program's by a relative error of at most 0.012.
Values may be sent and summed in bfloat16 or wider, within the bound.
A program may use at most 64 MiB of HBM per device.

v0:
```python
from functools import partial
import math

import jax
import jax.numpy as jnp
from jax import lax
from jax.sharding import PartitionSpec as P

BLOCK = 128


def slot_layout(block_rows, groups, per_group, capacity):
    head_count, segments, listed = block_rows.shape
    ordered = jnp.transpose(block_rows, (2, 0, 1)).reshape(-1)
    head_ids = jnp.broadcast_to(
        jnp.arange(head_count, dtype=jnp.int32)[None, :, None], (listed, head_count, segments)
    ).reshape(-1)
    owners = ordered // per_group
    req_codes = head_ids * per_group + ordered % per_group
    positions = jnp.arange(ordered.shape[0], dtype=jnp.int32)
    earlier = (owners[:, None] == owners[None, :]) & (positions[None, :] < positions[:, None])
    places = owners * capacity + jnp.sum(earlier.astype(jnp.int32), axis=1)
    targets = jnp.arange(groups * capacity, dtype=jnp.int32)
    matched = places[None, :] == targets[:, None]
    filled = jnp.any(matched, axis=1)
    source_ids = jnp.sum(jnp.where(matched, positions[None, :], 0), axis=1)
    sent_codes = jnp.where(filled, jnp.sum(jnp.where(matched, req_codes[None, :], 0), axis=1), -1)
    return (places, filled, source_ids, sent_codes.reshape(groups, capacity))


def log_total(scores, sink_grp):
    sink_side = sink_grp[:, None, None]
    row_top = jnp.maximum(jnp.max(scores, axis=-1), sink_side)
    row_total = jnp.exp(sink_side - row_top) + jnp.sum(
        jnp.exp(scores - row_top[..., None]), axis=-1
    )
    return row_top + jnp.log(row_total)


def forward_group(inputs, scaling):
    query_grp, local_kv, remote_kv, sink_grp = inputs
    head_dim = query_grp.shape[-1]
    kv_all = jnp.concatenate([local_kv, remote_kv], axis=2)
    scores = (
        jnp.einsum(
            "gsqd,gskd->gsqk", query_grp, kv_all[..., :head_dim], preferred_element_type=jnp.float32
        )
        * scaling
    )
    log_norm = log_total(scores, sink_grp)
    prob_bf = jnp.exp(scores - log_norm[..., None]).astype(jnp.bfloat16)
    attended = jnp.einsum(
        "gsqk,gskd->gsqd", prob_bf, kv_all[..., head_dim:], preferred_element_type=jnp.float32
    )
    return (attended.astype(jnp.bfloat16), log_norm)


def backward_group(inputs, scaling, seg_len):
    query_grp, local_kv, remote_kv, sink_grp, grad_grp, attended, log_norm = inputs
    head_dim = query_grp.shape[-1]
    kv_all = jnp.concatenate([local_kv, remote_kv], axis=2)
    scores = (
        jnp.einsum(
            "gsqd,gskd->gsqk", query_grp, kv_all[..., :head_dim], preferred_element_type=jnp.float32
        )
        * scaling
    )
    weights = jnp.exp(scores - log_norm[..., None])
    prob_bf = weights.astype(jnp.bfloat16)
    row_delta = jnp.sum(grad_grp.astype(jnp.float32) * attended.astype(jnp.float32), axis=-1)
    dprobs = jnp.einsum(
        "gsqd,gskd->gsqk", grad_grp, kv_all[..., head_dim:], preferred_element_type=jnp.float32
    )
    dscores = (weights * (dprobs - row_delta[..., None])).astype(jnp.bfloat16)
    grad_q = (
        jnp.einsum(
            "gsqk,gskd->gsqd", dscores, kv_all[..., :head_dim], preferred_element_type=jnp.float32
        )
        * scaling
    )
    key_terms = (
        jnp.einsum("gsqk,gsqd->gskd", dscores, query_grp, preferred_element_type=jnp.float32)
        * scaling
    )
    value_terms = jnp.einsum(
        "gsqk,gsqd->gskd", prob_bf, grad_grp, preferred_element_type=jnp.float32
    )
    all_terms = jnp.concatenate([key_terms, value_terms], axis=-1)
    sink_part = -jnp.sum(jnp.exp(sink_grp[:, None, None] - log_norm) * row_delta, axis=(1, 2))
    return (
        grad_q.astype(jnp.bfloat16),
        all_terms[:, :, :seg_len],
        all_terms[:, :, seg_len:].astype(jnp.bfloat16),
        sink_part,
    )


def body(query_in, key_in, value_in, grad_out, key_blocks, sink_logits):
    groups = lax.axis_size("ctx")
    head_count = sink_logits.shape[0]
    tok_dev = query_in.shape[1]
    head_dim = query_in.shape[2] // head_count
    seg_per_dev = key_blocks.shape[1]
    listed = key_blocks.shape[2]
    seg_len = tok_dev // seg_per_dev
    per_group = tok_dev // BLOCK
    requests = head_count * seg_per_dev * listed
    capacity = (requests + groups - 2) // (groups - 1)
    scaling = 1.0 / math.sqrt(head_dim)
    pair_heads = 2
    pair_count = head_count // pair_heads
    double_dim = 2 * head_dim
    places, filled, source_ids, sent_codes = slot_layout(key_blocks, groups, per_group, capacity)
    recv_codes = lax.all_to_all(sent_codes, "ctx", split_axis=0, concat_axis=0, tiled=True)
    local_kv = jnp.concatenate(
        [
            key_in[0].reshape(per_group, BLOCK, head_count, head_dim),
            value_in[0].reshape(per_group, BLOCK, head_count, head_dim),
        ],
        axis=-1,
    )
    safe_codes = jnp.maximum(recv_codes, 0)
    payload = local_kv[safe_codes % per_group, :, safe_codes // per_group, :]

    def arrange_remote(fetched):
        flat_slots = fetched.reshape(groups * capacity, BLOCK, double_dim)
        remote_rows = flat_slots[places].reshape(listed, head_count, seg_per_dev, BLOCK, double_dim)
        remote_rows = jnp.transpose(remote_rows, (1, 2, 0, 3, 4))
        return remote_rows.reshape(pair_count, pair_heads, seg_per_dev, listed * BLOCK, double_dim)

    def to_pairs(field):
        columns = field.shape[-1]
        split = jnp.transpose(
            field.reshape(seg_per_dev, seg_len, head_count, columns), (2, 0, 1, 3)
        )
        return split.reshape(pair_count, pair_heads, seg_per_dev, seg_len, columns)

    fetched = lax.all_to_all(payload, "ctx", split_axis=0, concat_axis=0, tiled=True)
    remote_pairs = arrange_remote(fetched)
    query_pairs = to_pairs(query_in[0].reshape(tok_dev, head_count, head_dim))
    grad_pairs = to_pairs(grad_out[0].reshape(tok_dev, head_count, head_dim))
    local_pairs = to_pairs(local_kv.reshape(tok_dev, head_count, double_dim))
    sink_pairs = sink_logits.reshape(pair_count, pair_heads)
    attended, log_norm = lax.map(
        partial(forward_group, scaling=scaling),
        (query_pairs, local_pairs, remote_pairs, sink_pairs),
    )
    back_remote = arrange_remote(
        lax.all_to_all(payload, "ctx", split_axis=0, concat_axis=0, tiled=True)
    )
    grad_q, own_terms, list_terms, sink_parts = lax.map(
        partial(backward_group, scaling=scaling, seg_len=seg_len),
        (query_pairs, local_pairs, back_remote, sink_pairs, grad_pairs, attended, log_norm),
    )
    grad_query = jnp.transpose(
        grad_q.reshape(head_count, seg_per_dev, seg_len, head_dim), (1, 2, 0, 3)
    )
    grad_query = grad_query.reshape(1, tok_dev, head_count * head_dim)
    own_flat = jnp.transpose(
        own_terms.reshape(head_count, seg_per_dev, seg_len, double_dim), (1, 2, 0, 3)
    )
    own_flat = own_flat.reshape(tok_dev, head_count, double_dim)
    list_rows = jnp.transpose(
        list_terms.reshape(head_count, seg_per_dev, listed, BLOCK, double_dim), (2, 0, 1, 3, 4)
    )
    list_rows = list_rows.reshape(requests, BLOCK, double_dim)
    send_back = jnp.where(filled[:, None, None], list_rows[source_ids], jnp.zeros((), jnp.bfloat16))
    returned = lax.all_to_all(
        send_back.reshape(groups, capacity, BLOCK, double_dim),
        "ctx",
        split_axis=0,
        concat_axis=0,
        tiled=True,
    )
    selector = (
        recv_codes.reshape(-1)[:, None]
        == jnp.arange(head_count * per_group, dtype=jnp.int32)[None, :]
    ).astype(jnp.bfloat16)
    incoming = jnp.einsum(
        "pj,pbe->jbe",
        selector,
        returned.reshape(groups * capacity, BLOCK, double_dim),
        preferred_element_type=jnp.float32,
    )
    incoming = jnp.transpose(
        incoming.reshape(head_count, per_group, BLOCK, double_dim), (1, 2, 0, 3)
    )
    combined = own_flat + incoming.reshape(tok_dev, head_count, double_dim)
    grad_key = (
        combined[..., :head_dim].astype(jnp.bfloat16).reshape(1, tok_dev, head_count * head_dim)
    )
    grad_value = (
        combined[..., head_dim:].astype(jnp.bfloat16).reshape(1, tok_dev, head_count * head_dim)
    )
    grad_sink = lax.psum(sink_parts.reshape(head_count), ("dp", "ctx"))
    return (grad_query, grad_key, grad_value, grad_sink)


def solution(mesh):
    placed = (
        P("dp", "ctx", None),
        P("dp", "ctx", None),
        P("dp", "ctx", None),
        P("dp", "ctx", None),
        P(None, "ctx", None),
        P(),
    )
    return jax.shard_map(
        body,
        mesh=mesh,
        in_specs=placed,
        out_specs=(P("dp", "ctx", None), P("dp", "ctx", None), P("dp", "ctx", None), P()),
        check_vma=False,
    )
```

profile of v0, /device:TPU:1, one launch (start us, length us, event | category | flops | bytes accessed | tf_op | source)
XLA Modules:
  0.0 473.0 jit_solution(14421471684461468160)
XLA Ops:
  2.7 10.5 %all-to-all-start = ((s32[32,1,2]{2,1,0:T(1,128)}), s32[32,1,2]{2,1,0:T(1,128)S(1)}, u32[]{:S(2)}, u32[]{:S(2)}) async-start(s32[32,1,2]{2,1,0:T(1,128)} %bitcast.31), calls=%async_computation | async-start | bytes 32768 | tf_op jit(solution)/shard_map/all_to_all | solution.py:114
  13.2 1.5 reshape.729
  15.6 6.1 %all-to-all-done = s32[32,1,2]{2,1,0:T(1,128)S(1)} async-done(((s32[32,1,2]{2,1,0:T(1,128)}), s32[32,1,2]{2,1,0:T(1,128)S(1)}, u32[]{:S(2)}, u32[]{:S(2)}) %all-to-all-start) | async-done | bytes 288 | tf_op jit(solution)/shard_map/all_to_all | solution.py:114
  22.0 2.8 gather_fusion
  24.8 5.0 %all-to-all-start.1 = ((bf16[32,2,128,256]{3,2,1,0:T(8,128)(2,1)}), bf16[32,2,128,256]{3,2,1,0:T(8,128)(2,1)}, u32[]{:S(2)}, u32[]{:S(2)}) async-start(bf16[32,2,128,256]{3,2,1,0:T(8,128)(2,1)} %bitcast.232), calls=%async_computation.1 | async-start | bytes 8388608 | tf_op jit(solution)/shard_map/all_to_all | solution.py:149
  31.1 1.1 copy.160
  32.2 2.2 copy.159
  34.5 1.5 copy.161
  36.0 86.5 %all-to-all-done.1 = bf16[32,2,128,256]{3,2,1,0:T(8,128)(2,1)} async-done(((bf16[32,2,128,256]{3,2,1,0:T(8,128)(2,1)}), bf16[32,2,128,256]{3,2,1,0:T(8,128)(2,1)}, u32[]{:S(2)}, u32[]{:S(2)}) %all-to-all-start.1) | async-done | bytes 4194336 | tf_op jit(solution)/shard_map/all_to_all | solution.py:149
  122.5 4.9 %gather_fusion.1 = bf16[60,128,256]{2,1,0:T(8,128)(2,1)} fusion(bf16[64,128,256]{2,1,0:T(8,128)(2,1)} %bitcast.36, s32[1024]{0:T(1024)S(1)} %pad_clamp_fusion.1), kind=kCustom, calls=%fused_computation.1 | custom fusion | bytes 7864560 | tf_op jit(solution)/shard_map/gather | solution.py:127
  127.4 4.4 copy.155
  131.8 28.0 %while.28 = (s32[]{:T(128)}, bf16[5,2,1,256,128]{4,3,1,2,0:T(8,128)(2,1)}, f32[5,2,1,256]{3,1,2,0:T(2,128)S(1)}, bf16[5,2,1,256,128]{4,3,1,2,0:T(8,128)(2,1)}, b...) while((s32[]{:T(128)}, ...), condition=%wide.region_6.7_spmd, body=%wide.region_3.6_spmd.sunk | while | flops 274796032 | bytes 10773141 | solution.py:144
  132.8 1.2 dynamic-slice_bitcast_fusion.9
  134.0 1.4 multiply_reduce_fusion.6
  136.1 1.2 fusion.95
  138.4 1.2 dynamic-slice_bitcast_fusion.9
  139.6 1.4 multiply_reduce_fusion.6
  141.7 1.2 fusion.95
  144.0 1.2 dynamic-slice_bitcast_fusion.9
  145.2 1.4 multiply_reduce_fusion.6
  147.3 1.2 fusion.95
  149.6 1.2 dynamic-slice_bitcast_fusion.9
  150.8 1.4 multiply_reduce_fusion.6
  152.9 1.2 fusion.95
  155.2 1.2 dynamic-slice_bitcast_fusion.9
  156.4 1.4 multiply_reduce_fusion.6
  158.5 1.2 fusion.95
  159.8 69.5 %while.29 = (s32[]{:T(128)}, bf16[5,2,1,256,128]{3,4,1,0,2:T(8,128)(2,1)}, f32[5,2,1,256,256]{3,4,1,2,0:T(8,128)}, bf16[5,2,1,768,256]{4,3,1,0,2:T(8,128)(2,1)},...) while((s32[]{:T(128)}, ...), condition=%wide.region_10.11_spmd, body=%wide.region_7.10_spmd.sunk | while | flops 680788992 | bytes 27408636 | solution.py:151
  160.9 1.1 multiply_reduce_fusion.7
  163.2 1.2 dynamic-slice_bitcast_fusion.11
  164.4 1.3 fusion.107
  167.5 1.3 fusion.110
  170.6 1.4 copy.191
  174.8 1.1 multiply_reduce_fusion.7
  177.1 1.2 dynamic-slice_bitcast_fusion.11
  178.3 1.3 fusion.107
  181.4 1.3 fusion.110
  184.5 1.4 copy.191
  188.7 1.1 multiply_reduce_fusion.7
  191.0 1.2 dynamic-slice_bitcast_fusion.11
  192.2 1.3 fusion.107
  195.3 1.3 fusion.110
  198.4 1.4 copy.191
  204.9 1.2 dynamic-slice_bitcast_fusion.11
  206.1 1.3 fusion.107
  209.2 1.3 fusion.110
  212.2 1.4 copy.191
  218.8 1.2 dynamic-slice_bitcast_fusion.11
  220.0 1.3 fusion.107
  223.1 1.3 fusion.110
  226.1 1.4 copy.191
  229.3 4.4 copy.166
  233.7 4.9 %gather_fusion.2 = bf16[64,128,256]{2,1,0:T(8,128)(2,1)} fusion(bf16[60,128,256]{2,1,0:T(8,128)(2,1)} %bitcast.231, s32[1024]{0:T(1024)S(1)} %pad_clamp_fusion), kind=kCustom, calls=%fused_computation.2 | custom fusion | bytes 8388864 | tf_op jit(solution)/shard_map/gather | solution.py:167
  238.6 9.1 %broadcast_select_fusion = bf16[32,2,128,256]{3,1,2,0:T(2,128)(2,1)} fusion(pred[32,2]{1,0:T(8,128)(4,1)S(1)} %broadcast_in_dim.98, bf16[32,2,128,256]{3,2,1,0:T(8,128)(2,1)} %bitcast.234), kind=kLoop, calls=%fused_computation.85 | loop fusion | flops 2097152 | bytes 8388672 | tf_op jit(solution)/shard_map/jit(_where)/select_n | solution.py:167
  247.7 6.8 %all-to-all-start.2 = ((bf16[32,2,128,256]{3,1,2,0:T(2,128)(2,1)}), bf16[32,2,128,256]{3,1,2,0:T(2,128)(2,1)}, u32[]{:S(2)}, u32[]{:S(2)}) async-start(bf16[32,2,128,256]{3,1,2,0:T(2,128)(2,1)} %broadcast_select_fusion), calls=%async_computation.2 | async-start | bytes 8388608 | tf_op jit(solution)/shard_map/all_to_all | solution.py:168
  255.9 186.1 %psum.7 = f32[10]{0:T(128)} all-reduce(f32[10]{0:T(128)S(1)} %reshape.704), channel_id=1, replica_groups=mesh['dp'=16,'ctx'=32] {'dp','ctx'}, use_global_device_ids=true, to_apply=%region_12.13 | all-reduce | flops 10 | bytes 80 | tf_op jit(solution)/shard_map/psum | solution.py:195
  442.0 2.2 copy.170
  444.1 8.9 %copy.168 = bf16[32,2,128,256]{3,1,0,2:T(2,128)(2,1)} copy(bf16[32,2,128,256]{3,1,2,0:T(2,128)(2,1)} %all-to-all-done.2) | data formatting | bytes 8388608 | tf_op jit(solution)/shard_map/all_to_all | solution.py:168
  453.0 7.2 %reshape.728 = bf16[64,128,256,1]{2,0,1,3:T(8,128)(2,1)} reshape(bf16[32,2,128,256]{3,1,0,2:T(2,128)(2,1)} %copy.168) | data formatting | bytes 8388608 | tf_op jit(solution)/shard_map/reshape | solution.py:182
  460.2 4.9 %fusion.56 = f32[10,2,128,256]{3,0,2,1:T(8,128)} fusion(bf16[64,128,256,1]{2,0,1,3:T(8,128)(2,1)} %reshape.728, s32[10,2]{0,1:T(2,128)S(1)} %multiply_add_fusion, s32[64]{0:T(128)S(1)} %eq.67), kind=kOutput, calls=%fused_computation.97 | convolution fusion | flops 83887360 | bytes 6816080 | tf_op jit(solution)/shard_map/pj,pbe->jbe/dot_general | solution.py:179
  465.2 3.4 copy.169
  468.6 2.2 fusion.53
  470.8 1.1 copy.172
  471.9 1.1 copy.171
  (162 shorter events, 54.6 us)
Async XLA Ops:
  0.6 0.7 copy-start
  0.6 14.2 %copy-start.3 = (bf16[1,256,1280]{2,1,0:T(8,128)(2,1)S(1)}, bf16[1,256,1280]{2,1,0:T(8,128)(2,1)}, u32[]{:S(2)}) copy-start(bf16[1,256,1280]{2,1,0:T(8,128)(2,1)} %param.12) | copy-start | bytes 1966084
  2.7 19.0 %all-to-all-start = ((s32[32,1,2]{2,1,0:T(1,128)}), s32[32,1,2]{2,1,0:T(1,128)S(1)}, u32[]{:S(2)}, u32[]{:S(2)}) async-start(s32[32,1,2]{2,1,0:T(1,128)} %bitcast.31), calls=%async_computation | async-start | bytes 32768 | tf_op jit(solution)/shard_map/all_to_all | solution.py:114
  24.8 5.2 %copy-start.2 = (bf16[1,256,1280]{2,1,0:T(8,128)(2,1)S(1)}, bf16[1,256,1280]{2,1,0:T(8,128)(2,1)}, u32[]{:S(2)}) copy-start(bf16[1,256,1280]{2,1,0:T(8,128)(2,1)} %param.11) | copy-start | bytes 1966084
  24.8 97.7 %all-to-all-start.1 = ((bf16[32,2,128,256]{3,2,1,0:T(8,128)(2,1)}), bf16[32,2,128,256]{3,2,1,0:T(8,128)(2,1)}, u32[]{:S(2)}, u32[]{:S(2)}) async-start(bf16[32,2,128,256]{3,2,1,0:T(8,128)(2,1)} %bitcast.232), calls=%async_computation.1 | async-start | bytes 8388608 | tf_op jit(solution)/shard_map/all_to_all | solution.py:149
  29.8 0.8 copy-start.5
  29.8 1.1 copy-start.4
  247.7 196.5 %all-to-all-start.2 = ((bf16[32,2,128,256]{3,1,2,0:T(2,128)(2,1)}), bf16[32,2,128,256]{3,1,2,0:T(2,128)(2,1)}, u32[]{:S(2)}, u32[]{:S(2)}) async-start(bf16[32,2,128,256]{3,1,2,0:T(2,128)(2,1)} %broadcast_select_fusion), calls=%async_computation.2 | async-start | bytes 8388608 | tf_op jit(solution)/shard_map/all_to_all | solution.py:168
  468.5 4.5 copy-start.1
where the time goes:
time: 476 us; the launch traced here: 473 us
  blocking collectives  186 us (39%)
  local copies, waits for them, and re-layouts  98.7 us (21%)
  waiting for transfers between devices  92.6 us (19%)
  matrix products  40.1 us (8%)
  other arithmetic  31.8 us (7%)
  starting transfers between devices  22.3 us (5%)
    psum x1, blocking collectives, body(): grad_sink = lax.psum(sink_parts.reshape(head_count), ('dp', 'ctx'))  186 us
    all_to_all x1, waiting for transfers between devices, body(): lax.all_to_all(payload, 'ctx', split_axis=0, concat_axis=0, tiled=True)  86.5 us
    squeeze x20, local copies, waits for them, and re-layouts, body(): lax.map(partial(forward_group, scaling=scaling), (query_pairs, local_pair...  21.6 us
    dynamic_update_slice x15, local copies, waits for them, and re-layouts, body(): lax.map(partial(backward_group, scaling=scaling, seg_len=seg_len), (query...  11.9 us
    all_to_all x1, starting transfers between devices, body(): lax.all_to_all(sent_codes, 'ctx', split_axis=0, concat_axis=0, tiled=True)  10.5 us
  transfers between devices with their start and end apart: 3, of which 2 were waited for; matrix products, arithmetic and copies ran while one was open for 2% of the time, Pallas kernels for 0%

commit v1 on v0

v1 whole, which is shorter than its diff:
```python
from functools import partial
import math

import jax
import jax.numpy as jnp
from jax import lax
from jax.experimental import pallas as pl
from jax.experimental.pallas import tpu as pltpu
from jax.sharding import PartitionSpec as P

BLOCK = 128
SEG = 256
HD = 128
HEADS = 10
NSEG = 32
HALF = NSEG // 2
LISTED = 6
ROWS = NSEG * SEG
HROWS = HALF * SEG
CHUNKS = 4
LOG2E = math.log2(math.e)
SCALE = 1.0 / math.sqrt(HD)
MESH = pl.DeviceIdType.MESH


def div(a, b):
    return lax.div(a, jnp.int32(b))


def rem(a, b):
    return lax.rem(a, jnp.int32(b))


def home_ctx(core, head):
    pair = core * HEADS + head
    j = div(pair, 5)
    r = rem(pair, 5)
    odd = div(r, 3)
    x = rem(r + j + 8 + odd * (r - 6), 4)
    return 4 * (2 * j + odd) + x


def my_pair(ctx):
    y = div(ctx, 4)
    j = div(y, 2)
    odd = rem(y, 2)
    u = rem(rem(ctx, 4) + 4 - j, 4)
    is_home = ((1 - odd) * div(u, 3) + odd * rem(u, 2)) == 0
    r = (1 - odd) * u + odd * (3 + div(u, 2))
    pair = 5 * j + r
    return is_home, div(pair, HEADS), rem(pair, HEADS)


class Place:
    def __init__(self):
        dp = lax.axis_index("dp")
        self.ctx = lax.axis_index("ctx")
        self.core = rem(dp, 2)
        self.plane = dp - self.core
        self.is_home, self.pair_core, self.pair_head = my_pair(self.ctx)
        self.target_core = 1 - div(self.ctx, HALF)
        self.half = 1 - self.core
        self.sibling = (self.plane + 1 - self.core, self.ctx)

    def home(self, head):
        return (self.plane + self.target_core, home_ctx(self.core, head))

    def owner(self, j):
        return (self.plane + self.pair_core, self.half * HALF + j)


def greet(place):
    barrier = pltpu.get_barrier_semaphore()

    @pl.loop(0, HEADS)
    def _(i):
        pl.semaphore_signal(barrier, inc=1, device_id=place.home(i), device_id_type=MESH)

    @pl.when(place.is_home)
    def _():
        @pl.loop(0, HALF)
        def _(j):
            pl.semaphore_signal(barrier, inc=1, device_id=place.owner(j), device_id_type=MESH)

        pl.semaphore_signal(barrier, inc=1, device_id=place.sibling, device_id_type=MESH)

    pl.semaphore_wait(barrier, HEADS + place.is_home.astype(jnp.int32) * (HALF + 1))


def columns(head):
    return pl.ds(pl.multiple_of(head * HD, HD), HD)


def rows_of(start, size):
    return pl.ds(pl.multiple_of(start, size), size)


def collect_kernel(
    q_in, k_in, v_in, g_in, lists_in, q_out, g_out, k_out, v_out, lists_out,
    send_sem, recv_sem, list_send, list_recv, swap_send, swap_recv,
):
    place = Place()
    greet(place)
    seg_rows = rows_of(place.ctx * SEG, SEG)
    loc_rows = rows_of(rem(place.ctx, HALF) * SEG, SEG)

    def remote(src, dst, ssem, rsem, target):
        return pltpu.make_async_remote_copy(
            src_ref=src, dst_ref=dst, send_sem=ssem, recv_sem=rsem,
            device_id=target, device_id_type=MESH,
        )

    @pl.loop(0, HEADS)
    def _(i):
        head = rem(place.ctx + i, HEADS)
        cols = columns(head)
        target = place.home(head)
        remote(k_in.at[0, :, cols], k_out.at[seg_rows], send_sem.at[0], recv_sem.at[0], target).start()
        remote(v_in.at[0, :, cols], v_out.at[seg_rows], send_sem.at[1], recv_sem.at[1], target).start()

    @pl.loop(0, HEADS)
    def _(i):
        head = rem(place.ctx + i, HEADS)
        cols = columns(head)
        target = place.home(head)
        remote(lists_in.at[head], lists_out.at[rem(place.ctx, HALF)], list_send, list_recv, target).start()
        remote(q_in.at[0, :, cols], q_out.at[loc_rows], send_sem.at[2], recv_sem.at[2], target).start()
        remote(g_in.at[0, :, cols], g_out.at[loc_rows], send_sem.at[3], recv_sem.at[3], target).start()

    @pl.when(place.is_home)
    def _():
        mine = rows_of(place.half * HROWS, HROWS)
        other = rows_of(place.core * HROWS, HROWS)
        for t, ref in enumerate((k_out, v_out)):
            part = ref.at[mine]
            remote(part, part, send_sem.at[t], recv_sem.at[t], place.sibling).wait_recv()
            remote(part, part, swap_send.at[t], swap_recv.at[t], place.sibling).start()
        remote(lists_out, lists_out, list_send, list_recv, place.sibling).wait_recv()
        remote(q_out, q_out, send_sem.at[2], recv_sem.at[2], place.sibling).wait_recv()
        remote(g_out, g_out, send_sem.at[3], recv_sem.at[3], place.sibling).wait_recv()
        for t, ref in enumerate((k_out, v_out)):
            remote(ref.at[mine], ref.at[other], swap_send.at[t], swap_recv.at[t], place.sibling).wait()

    remote(lists_in, lists_in, list_send, list_recv, place.sibling).wait_send()
    for t, ref in enumerate((k_in, v_in, q_in, g_in)):
        remote(ref, ref, send_sem.at[t], recv_sem.at[t], place.sibling).wait_send()


def fold(x, op):
    return op(x.reshape(x.shape[0] // 8, 8, x.shape[1]), axis=0)


NT = (((1,), (1,)), ((), ()))
TN = (((0,), (0,)), ((), ()))


def attend_kernel(
    lists, sinks, q_ref, g_ref, k_ref, v_ref,
    dq_ref, own_k, own_v, far_k, far_v, sink_out,
    e_ref, p_ref, acc_k, acc_v,
):
    sink_out[...] = jnp.zeros_like(sink_out)
    place = Place()

    @pl.when(place.is_home)
    def _():
        half = place.half
        sink2 = sinks[place.pair_head] * LOG2E
        acc_k[...] = jnp.zeros_like(acc_k)
        acc_v[...] = jnp.zeros_like(acc_v)

        @pl.loop(0, HALF)
        def _(j):
            q = q_ref[rows_of(j * SEG, SEG), :]
            g = g_ref[rows_of(j * SEG, SEG), :]
            spans = [(rows_of((half * HALF + j) * SEG, SEG), 0, SEG)]
            for m in range(LISTED):
                spans.append((rows_of(lists[j, 0, m] * BLOCK, BLOCK), SEG + m * BLOCK, BLOCK))
            top8 = None
            for src, at, size in spans:
                s = lax.dot_general(k_ref[src, :], q, NT, preferred_element_type=jnp.float32)
                e_ref[at:at + size, :] = s
                high = fold(s, jnp.max)
                top8 = high if top8 is None else jnp.maximum(top8, high)
            factor = SCALE * LOG2E
            top = jnp.maximum(jnp.max(top8, axis=0, keepdims=True) * factor, sink2)
            sum8 = jnp.zeros((8, SEG), jnp.float32)
            dot8 = jnp.zeros((8, SEG), jnp.float32)
            for src, at, size in spans:
                dp = lax.dot_general(v_ref[src, :], g, NT, preferred_element_type=jnp.float32)
                e = jnp.exp2(e_ref[at:at + size, :] * factor - top)
                e_ref[at:at + size, :] = e
                p_ref[at:at + size, :] = dp
                sum8 = sum8 + fold(e, jnp.sum)
                dot8 = dot8 + fold(e * dp, jnp.sum)
            sink_e = jnp.exp2(sink2 - top)
            total = sink_e + jnp.sum(sum8, axis=0, keepdims=True)
            inv = 1.0 / total
            delta = jnp.sum(dot8, axis=0, keepdims=True) * inv
            sink_out[...] = sink_out[...] - sink_e * inv * delta
            dq_t = jnp.zeros((HD, SEG), jnp.float32)
            for src, at, size in spans:
                w = e_ref[at:at + size, :] * inv
                ds = (w * (p_ref[at:at + size, :] - delta)).astype(jnp.bfloat16)
                w = w.astype(jnp.bfloat16)
                acc_v[src, :] += jnp.dot(w, g, preferred_element_type=jnp.float32)
                acc_k[src, :] += jnp.dot(ds, q, preferred_element_type=jnp.float32)
                dq_t = dq_t + lax.dot_general(k_ref[src, :], ds, TN, preferred_element_type=jnp.float32)
            dq_ref[rows_of(j * SEG, SEG), :] = (dq_t * SCALE).T.astype(jnp.bfloat16)

        mine = rows_of(half * HROWS, HROWS)
        other = rows_of((1 - half) * HROWS, HROWS)
        own_k[...] = acc_k[mine, :] * SCALE
        own_v[...] = acc_v[mine, :]
        far_k[...] = (acc_k[other, :] * SCALE).astype(jnp.bfloat16)
        far_v[...] = acc_v[other, :].astype(jnp.bfloat16)


def return_kernel(
    dq, own_k, own_v, far_k, far_v, gq, gk, gv, near_k, near_v, fin_k, fin_v,
    send_sem, recv_sem, swap_send, swap_recv,
):
    place = Place()
    greet(place)

    def remote(src, dst, ssem, rsem, target):
        return pltpu.make_async_remote_copy(
            src_ref=src, dst_ref=dst, send_sem=ssem, recv_sem=rsem,
            device_id=target, device_id_type=MESH,
        )

    step = HROWS // CHUNKS
    pairs = ((far_k, near_k, own_k, fin_k, gk), (far_v, near_v, own_v, fin_v, gv))

    @pl.when(place.is_home)
    def _():
        cols = columns(place.pair_head)
        for c in range(CHUNKS):
            part = pl.ds(c * step, step)
            for t, (far, near, _, _, _) in enumerate(pairs):
                remote(far.at[part], near.at[part], swap_send.at[t, c], swap_recv.at[t, c], place.sibling).start()

        @pl.loop(0, HALF)
        def _(i):
            j = rem(place.ctx + i, HALF)
            rows = rows_of(j * SEG, SEG)
            remote(dq.at[rows], gq.at[0, :, cols], send_sem.at[2], recv_sem.at[2], place.owner(j)).start()

        for c in range(CHUNKS):
            part = pl.ds(c * step, step)
            for t, (far, near, own, fin, out) in enumerate(pairs):
                remote(far.at[part], near.at[part], swap_send.at[t, c], swap_recv.at[t, c], place.sibling).wait()
                fin[part, :] = (own[part, :] + near[part, :].astype(jnp.float32)).astype(jnp.bfloat16)

                @pl.loop(0, HALF // CHUNKS)
                def _(i):
                    j = c * (HALF // CHUNKS) + i
                    rows = rows_of(j * SEG, SEG)
                    remote(fin.at[rows], out.at[0, :, cols], send_sem.at[t], recv_sem.at[t], place.owner(j)).start()

        remote(fin_k, fin_k, send_sem.at[0], recv_sem.at[0], place.sibling).wait_send()
        remote(fin_v, fin_v, send_sem.at[1], recv_sem.at[1], place.sibling).wait_send()
        remote(dq, dq, send_sem.at[2], recv_sem.at[2], place.sibling).wait_send()

    for t, ref in enumerate((gk, gv, gq)):
        remote(ref, ref, send_sem.at[t], recv_sem.at[t], place.sibling).wait_recv()


def body(query_in, key_in, value_in, grad_out, key_blocks, sink_logits):
    bf16, f32 = jnp.bfloat16, jnp.float32
    any_spec = pl.BlockSpec(memory_space=pl.ANY)
    vmem_spec = pl.BlockSpec(memory_space=pltpu.VMEM)
    smem_spec = pl.BlockSpec(memory_space=pltpu.SMEM)
    dma = pltpu.SemaphoreType.DMA
    shape = jax.ShapeDtypeStruct
    lists = jnp.pad(key_blocks, ((0, 0), (0, 0), (0, BLOCK - LISTED)))
    q_all, g_all, k_all, v_all, lists_all = pl.pallas_call(
        collect_kernel,
        out_shape=(
            shape((HROWS, HD), bf16), shape((HROWS, HD), bf16),
            shape((ROWS, HD), bf16), shape((ROWS, HD), bf16),
            shape((HALF, 1, BLOCK), jnp.int32),
        ),
        in_specs=[any_spec] * 5,
        out_specs=(any_spec,) * 5,
        scratch_shapes=[dma((4,)), dma((4,)), dma, dma, dma((2,)), dma((2,))],
        compiler_params=pltpu.CompilerParams(collective_id=0, has_side_effects=True),
        name="collect",
    )(query_in, key_in, value_in, grad_out, lists)

    place = Place()
    dq, own_k, own_v, far_k, far_v, sink_part = pl.pallas_call(
        attend_kernel,
        out_shape=(
            shape((HROWS, HD), bf16), shape((HROWS, HD), f32), shape((HROWS, HD), f32),
            shape((HROWS, HD), bf16), shape((HROWS, HD), bf16), shape((1, SEG), f32),
        ),
        in_specs=[smem_spec] * 2 + [vmem_spec] * 4,
        out_specs=(vmem_spec,) * 6,
        scratch_shapes=[
            pltpu.VMEM((SEG + LISTED * BLOCK, SEG), f32), pltpu.VMEM((SEG + LISTED * BLOCK, SEG), f32),
            pltpu.VMEM((ROWS, HD), f32), pltpu.VMEM((ROWS, HD), f32),
        ],
        compiler_params=pltpu.CompilerParams(vmem_limit_bytes=50 * 2**20),
        name="attend",
    )(lists_all, sink_logits, q_all, g_all, k_all, v_all)

    sink_vec = jnp.where(
        (jnp.arange(HEADS) == place.pair_head) & place.is_home, jnp.sum(sink_part), 0.0
    )
    grad_sink = lax.psum(sink_vec, ("dp", "ctx"))

    tok = query_in.shape
    gq, gk, gv = pl.pallas_call(
        return_kernel,
        out_shape=(shape(tok, bf16),) * 3,
        in_specs=[any_spec, vmem_spec, vmem_spec, any_spec, any_spec],
        out_specs=(any_spec,) * 3,
        scratch_shapes=[
            pltpu.VMEM((HROWS, HD), bf16), pltpu.VMEM((HROWS, HD), bf16),
            pltpu.VMEM((HROWS, HD), bf16), pltpu.VMEM((HROWS, HD), bf16),
            dma((3,)), dma((3,)), dma((2, CHUNKS)), dma((2, CHUNKS)),
        ],
        compiler_params=pltpu.CompilerParams(
            collective_id=1, has_side_effects=True, vmem_limit_bytes=40 * 2**20
        ),
        name="give_back",
    )(dq, own_k, own_v, far_k, far_v)
    return (gq, gk, gv, grad_sink)


def solution(mesh):
    placed = (
        P("dp", "ctx", None),
        P("dp", "ctx", None),
        P("dp", "ctx", None),
        P("dp", "ctx", None),
        P(None, "ctx", None),
        P(),
    )
    return jax.shard_map(
        body,
        mesh=mesh,
        in_specs=placed,
        out_specs=(P("dp", "ctx", None), P("dp", "ctx", None), P("dp", "ctx", None), P()),
        check_vma=False,
    )
```

time: 476 us -> 292 us (0.61)
  Pallas kernels: 0 us -> 166 us
  waiting for transfers between devices: 92.6 us -> 0 us
  local copies, waits for them, and re-layouts: 98.7 us -> 7.76 us
  blocking collectives: 186 us -> 115 us
  matrix products: 40.1 us -> 0 us
  other arithmetic: 31.8 us -> 1.25 us
  starting transfers between devices: 22.3 us -> 0 us
    pallas_call x0 -> x3, Pallas kernels: none -> 166 us  [the longest x1 71.4 us: body(): pl.pallas_call(return_kernel, out_shape=(shape(tok, bf16),) * 3, in_specs...]
    all_to_all x3 -> x0, waiting for transfers between devices: 92.6 us -> none  [the longest x1 86.5 us: body(): lax.all_to_all(payload, 'ctx', split_axis=0, concat_axis=0, tiled=True)]
    psum x1, blocking collectives: 186 us -> 115 us  [body(): grad_sink = lax.psum(sink_vec, ('dp', 'ctx'))]
    dot_general x36 -> x0, matrix products: 40.1 us -> none  [the longest x5 7.12 us: forward_group(): jnp.einsum('gsqd,gskd->gsqk', query_grp, kv_all[..., :head_dim], preferre...]
    all_to_all x3 -> x0, starting transfers between devices: 22.3 us -> none  [the longest x1 10.5 us: body(): lax.all_to_all(sent_codes, 'ctx', split_axis=0, concat_axis=0, tiled=True)]
    squeeze x20 -> x0, local copies, waits for them, and re-layouts: 21.6 us -> none  [body(): lax.map(partial(forward_group, scaling=scaling), (query_pairs, local_pair...]
    dynamic_update_slice x25 -> x0, local copies, waits for them, and re-layouts: 15.9 us -> none  [the longest x15 11.9 us: body(): lax.map(partial(backward_group, scaling=scaling, seg_len=seg_len), (query...]
    gather x3 -> x0, local copies, waits for them, and re-layouts: 12.5 us -> none  [the longest x1 4.88 us: arrange_remote(): flat_slots[places]]
  transfers between devices with their start and end apart: 3 -> 0, of which waited for: 2 -> 0; matrix products, arithmetic and copies ran while one was open for 2% -> 0% of each run, Pallas kernels for 0% -> 0%
where the time goes in v1:
time: 292 us; the launch traced here: 291 us
  Pallas kernels  166 us (57%)
  blocking collectives  115 us (39%)
  local copies, waits for them, and re-layouts  7.76 us (3%)
    psum x1, blocking collectives, body(): grad_sink = lax.psum(sink_vec, ('dp', 'ctx'))  115 us
    pallas_call x1, Pallas kernels, body(): pl.pallas_call(return_kernel, out_shape=(shape(tok, bf16),) * 3, in_specs...  71.4 us
    pallas_call x1, Pallas kernels, body(): pl.pallas_call(collect_kernel, out_shape=(shape((HROWS, HD), bf16), shape...  67.6 us
    pallas_call x1, Pallas kernels, body(): pl.pallas_call(attend_kernel, out_shape=(shape((HROWS, HD), bf16), shape(...  27.2 us
    unnamed x12, local copies, waits for them, and re-layouts  7.16 us

profile of v1, /device:TPU:1, one launch (start us, length us, event | category | flops | bytes accessed | tf_op | source)
XLA Modules:
  0.0 291.4 jit_solution(14771704381257939011)
XLA Ops:
  0.6 0.0 copy-start.3
  0.6 0.8 copy.10
  1.4 0.6 pad.4.lists_in
  2.0 67.6 %collect.1 = (bf16[4096,128]{1,0:T(8,128)(2,1)}, bf16[4096,128]{1,0:T(8,128)(2,1)}, bf16[8192,128]{1,0:T(8,128)(2,1)}, bf16[8192,128]{1,0:T(8,128)(2,1)}, s32[16,1,128]{2,1,0:T(1,128)}) custom-call(bf16[1,256,1280]{2,1,0:T(8,128)(2,1)} %q_in.1, bf16[1,256,1280]{2,1,0:T(8,128)(2,1)} %k_in.1, bf16[1,256,1280]{2,1,0:T(8,128)(2,1)} %v_in.1, ...), custom_call_target="tpu_custom_call" | custom-call | tf_op jit(solution)/shard_map/collect/pallas_call | solution.py:277
  69.6 0.0 copy-done.3
  69.6 0.0 copy-start.2
  69.7 0.7 copy-done.2
  70.3 27.2 %attend.1 = (bf16[4096,128]{1,0:T(8,128)(2,1)S(1)}, f32[4096,128]{1,0:T(8,128)}, f32[4096,128]{1,0:T(8,128)}, bf16[4096,128]{1,0:T(8,128)(2,1)S(1)}, bf16[4096,1...) custom-call(s32[16,1,128]{2,1,0:T(1,128)S(1)} %copy-done.2, f32[10]{0:T(128)S(1)} %copy-done.3, ...), custom_call_target="tpu_custom_call" | custom-call | tf_op jit(solution)/shard_map/attend/pallas_call | solution.py:292
  97.5 0.0 copy-start
  97.5 1.6 copy-done
  99.1 0.0 copy-start.1
  99.1 1.6 copy-done.1
  100.7 71.4 %give_back.1 = (bf16[1,256,1280]{2,1,0:T(8,128)(2,1)S(1)}, bf16[1,256,1280]{2,1,0:T(8,128)(2,1)S(1)}, bf16[1,256,1280]{2,1,0:T(8,128)(2,1)S(1)}) custom-call(bf16[4096,128]{1,0:T(8,128)(2,1)S(1)} %get-tuple-element.23.dq, f32[4096,128]{1,0:T(8,128)S(1)} %copy-done, f32[4096,128]{1,0:T(8,128)S(1)} %copy-done.1, ...), custom_call_target="tpu_custom_call" | custom-call | tf_op jit(solution)/shard_map/give_back/pallas_call | solution.py:314
  172.2 0.6 reduce_sum.9
  172.8 0.6 and_select_fusion
  173.4 115.4 %psum.7 = f32[10]{0:T(128)} all-reduce(f32[10]{0:T(128)S(1)} %and_select_fusion), channel_id=1, replica_groups=mesh['dp'=16,'ctx'=32] {'dp','ctx'}, use_global_device_ids=true, to_apply=%region_1.2 | all-reduce | flops 10 | bytes 80 | tf_op jit(solution)/shard_map/psum | solution.py:311
  288.9 0.8 copy.14
  289.7 0.8 copy.15
  290.5 0.8 copy.16
Async XLA Ops:
  0.6 69.0 %copy-start.3 = (f32[10]{0:T(128)S(1)}, f32[10]{0:T(128)}, u32[]{:S(2)}) copy-start(f32[10]{0:T(128)} %sinks.1) | copy-start | bytes 124
  69.6 0.7 copy-start.2
  97.5 1.6 copy-start
  99.1 1.6 copy-start.1

commit v2 on v1

v2 whole, which is shorter than its diff:
```python
import math

import jax
import jax.numpy as jnp
from jax import lax
from jax.experimental import pallas as pl
from jax.experimental.pallas import tpu as pltpu
from jax.sharding import PartitionSpec as P

BLOCK = 128
SEG = 256
HD = 128
HEADS = 10
NSEG = 32
HALF = NSEG // 2
LISTED = 6
KEYS = SEG + LISTED * BLOCK
SLOT = 8
EMPTY = 6
CHUNKS = 4
EARLY = 10
PLANES = 8
LOG2E = math.log2(math.e)
SCALE = 1.0 / math.sqrt(HD)
MESH = pl.DeviceIdType.MESH
F32 = jnp.float32
BF16 = jnp.bfloat16
NT = (((1,), (1,)), ((), ()))
TN = (((0,), (0,)), ((), ()))


def div(a, b):
    return lax.div(a, jnp.int32(b))


def rem(a, b):
    return lax.rem(a, jnp.int32(b))


def home_ctx(core, head):
    j = 2 * div(head, 5) + core
    r = rem(head, 5)
    odd = div(r, 3)
    x = rem(r + j + 8 + odd * (r - 6), 4)
    return 4 * (2 * j + odd) + x


def my_pair(ctx):
    y = div(ctx, 4)
    j = div(y, 2)
    odd = rem(y, 2)
    u = rem(rem(ctx, 4) + 4 - j, 4)
    is_home = ((1 - odd) * div(u, 3) + odd * rem(u, 2)) == 0
    r = (1 - odd) * u + odd * (3 + div(u, 2))
    return is_home, rem(j, 2), 5 * div(j, 2) + r


def half_of(s):
    return rem(div(s, 8), 2)


def local_of(s):
    return 8 * div(s, HALF) + rem(s, 8)


def segment(half, j):
    return HALF * div(j, 8) + 8 * half + rem(j, 8)


def is_spare(y, x):
    u = rem(x + 4 - div(y, 2), 4)
    odd = rem(y, 2)
    return ((1 - odd) * div(u, 3) + odd * rem(u, 2)) == 1


def turn(head, j):
    m = rem(div(8 * head, 5) + HALF - j, HALF)
    return 2 * rem(m, HALF // 2) + div(m, HALF // 2)


def taken(head, n):
    m = div(n, 2) + (HALF // 2) * rem(n, 2)
    return rem(div(8 * head, 5) + HALF - m, HALF)


class Place:
    def __init__(self):
        dp = lax.axis_index("dp")
        self.ctx = lax.axis_index("ctx")
        self.core = rem(dp, 2)
        self.plane = dp - self.core
        self.is_home, self.pair_core, self.pair_head = my_pair(self.ctx)
        self.target_core = 1 - half_of(self.ctx)
        self.half = 1 - self.core
        self.local = local_of(self.ctx)
        self.first = rem(div(5 * self.local + 7, 8), HEADS)
        self.sibling = (self.plane + 1 - self.core, self.ctx)
        self.y = div(self.ctx, 4)
        self.x = rem(self.ctx, 4)
        self.odd = rem(self.y, 2)
        self.spares = 1 + self.odd
        self.homes = 3 - self.odd
        self.row_head = 5 * div(self.y, 4) + 3 * self.odd
        self.row_core = rem(div(self.y, 2), 2)
        self.inside = (self.row_core == self.half).astype(jnp.int32)
        twin = home_ctx(1 - self.pair_core, self.pair_head)
        self.twins = ((self.plane, twin), (self.plane + 1, twin))

    def home(self, head):
        return (self.plane + self.target_core, home_ctx(self.core, head))

    def sent_to(self, i):
        return rem(self.first + div(i, 2) + (HEADS // 2) * rem(i, 2), HEADS)

    def owner(self, j):
        return (self.plane + self.pair_core, segment(self.half, j))

    def row_home(self, i):
        head = self.row_head + i
        return head, (self.plane + self.core, home_ctx(self.row_core, head))

    def relayed(self, j):
        x = rem(j, 4)
        device = (self.plane + self.core, 4 * self.y + x)
        return is_spare(self.y, x) & (div(segment(self.half, j), 4) != self.y), device

    def other_plane(self, i):
        return (rem(self.plane + self.core + 2 * i, 2 * PLANES), self.ctx)


def greet(place):
    barrier = pltpu.get_barrier_semaphore()

    def signal(device):
        pl.semaphore_signal(barrier, inc=1, device_id=device, device_id_type=MESH)

    @pl.loop(0, HEADS)
    def _(i):
        signal(place.home(i))

    @pl.loop(0, 4)
    def _(i):
        y = 4 * div(i, 2) + 2 * place.core + rem(i, 2)

        @pl.when(is_spare(y, place.x) & (y != place.y))
        def _():
            signal((place.plane + place.target_core, 4 * y + place.x))

    @pl.when(jnp.logical_not(place.is_home))
    def _():
        @pl.loop(0, place.homes)
        def _(i):
            signal(place.row_home(i)[1])

    @pl.when(place.is_home)
    def _():
        @pl.loop(0, HALF)
        def _(j):
            signal(place.owner(j))

        signal(place.sibling)
        for twin in place.twins:
            signal(twin)

        @pl.loop(1, PLANES)
        def _(i):
            signal(place.other_plane(i))

    home = place.is_home.astype(jnp.int32)
    peers = HALF + 1 + 2 + PLANES - 1 + place.spares
    pl.semaphore_wait(barrier, HEADS + home * peers + (1 - home) * (4 - place.inside))


def remote(src, dst, ssem, rsem, target):
    return pltpu.make_async_remote_copy(
        src_ref=src, dst_ref=dst, send_sem=ssem, recv_sem=rsem,
        device_id=target, device_id_type=MESH,
    )


def columns(head):
    return pl.ds(pl.multiple_of(head * HD, HD), HD)


def rows_of(start, size):
    return pl.ds(pl.multiple_of(start, size), size)


def fold(x, op):
    return op(x.reshape(x.shape[0] // 8, 8, x.shape[1]), axis=0)


def highest(x):
    part = x[0:8]
    for i in range(8, x.shape[0], 8):
        part = jnp.maximum(part, x[i:i + 8])
    row = part[0:1]
    for i in range(1, 8):
        row = jnp.maximum(row, part[i:i + 1])
    return row


def write_tables(lists, table):
    row = lists[0]
    for j in range(1, HALF):
        row = row + lists[j]
    row = row - 1
    shape = (BLOCK, BLOCK)
    wide = jnp.broadcast_to(row, shape)
    tall = wide.T
    entry = lax.broadcasted_iota(jnp.int32, shape, 0)
    lane = lax.broadcasted_iota(jnp.int32, shape, 1)
    before = highest(jnp.where((tall == wide) & (entry < lane), entry, -1))
    last = highest(jnp.where(tall == lane, entry, -1))
    place = jnp.maximum(row, 0)
    block = lax.bitwise_and(place, 1)
    s = lax.shift_right_logical(place, 1)
    half = lax.bitwise_and(lax.shift_right_logical(s, 3), 1)
    local = 8 * lax.shift_right_logical(s, 4) + lax.bitwise_and(s, 7)
    table[0:1, :] = 4 * (half * HALF + local) + block
    table[1:2, :] = jnp.where(before < 0, EMPTY, before)
    table[2:3, :] = jnp.where(last < 0, EMPTY, last)


def fused_kernel(
    q_in, k_in, v_in, g_in, lists_in, sinks, gq, gk, gv, sink_out,
    kv, qg, lists, table, entries, dq, term_k, term_v, own_k, own_v, far, near, fin, e_ref, p_ref,
    sink_sum, sink_a, sink_b, sink_c,
    list_send, list_recv, kv_send, kv_recv, swap_send, swap_recv, qg_send, qg_recv, dq_send, fin_send,
    relay_dq, relay_kv, relay_dq_recv, relay_kv_recv, relay_send,
    out_recv, far_send, far_recv, a_send, a_recv, b_send, b_recv, c_send, c_recv, table_sem,
):
    place = Place()
    greet(place)
    head_of = place.pair_head

    @pl.loop(0, HEADS)
    def _(i):
        head = place.sent_to(i)
        target = place.home(head)
        remote(lists_in.at[head], lists.at[place.local], list_send, list_recv, target).start()

    @pl.loop(0, HEADS)
    def _(i):
        head = place.sent_to(i)
        cols = columns(head)
        target = place.home(head)
        at = 4 * ((1 - place.target_core) * HALF + place.local)
        sem = kv_recv.at[place.local]
        remote(k_in.at[:, :, cols], kv.at[pl.ds(at, 2)], kv_send.at[0], sem, target).start()
        remote(v_in.at[:, :, cols], kv.at[pl.ds(at + 2, 2)], kv_send.at[1], sem, target).start()

    def pass_on(start, stop):
        @pl.loop(start, stop)
        def _(n):
            j = taken(head_of, n)
            part = kv.at[pl.ds(4 * (place.half * HALF + j), 4)]
            remote(part, part, kv_send.at[0], kv_recv.at[j], place.sibling).wait_recv()
            remote(part, part, swap_send, swap_recv, place.sibling).start()

    @pl.when(place.is_home)
    def _():
        remote(lists, lists, list_send, list_recv, place.sibling).wait_recv()
        write_tables(lists, table)
        down = pltpu.make_async_copy(table, entries, table_sem)
        down.start()
        term_k[EMPTY] = jnp.zeros((BLOCK, HD), F32)
        term_v[EMPTY] = jnp.zeros((BLOCK, HD), F32)
        sink_sum[...] = jnp.zeros_like(sink_sum)
        down.wait()

        pass_on(0, EARLY)

    for t, ref in enumerate((k_in, v_in)):
        remote(ref, ref, kv_send.at[t], kv_recv.at[0], place.sibling).wait_send()

    @pl.loop(0, HEADS)
    def _(i):
        head = place.sent_to(i)
        cols = columns(head)
        target = place.home(head)
        at = place.local * (2 * SEG)
        sem = qg_recv.at[place.local]
        remote(q_in.at[0, :, cols], qg.at[rows_of(at, SEG)], qg_send.at[0], sem, target).start()
        remote(g_in.at[0, :, cols], qg.at[rows_of(at + SEG, SEG)], qg_send.at[1], sem, target).start()

    @pl.when(place.is_home)
    def _():
        cols = columns(head_of)
        pass_on(EARLY, HALF)
        mine = kv.at[pl.ds(place.half * (4 * HALF), 4 * HALF)]
        other = kv.at[pl.ds(place.core * (4 * HALF), 4 * HALF)]
        remote(mine, other, swap_send, swap_recv, place.sibling).wait()
        sink2 = sinks[head_of] * LOG2E

        @pl.loop(0, HALF)
        def _(n):
            j = taken(head_of, n)
            part = qg.at[rows_of(j * (2 * SEG), 2 * SEG)]
            remote(part, part, qg_send.at[0], qg_recv.at[j], place.sibling).wait_recv()
            q = qg[rows_of(j * (2 * SEG), SEG), :]
            g = qg[rows_of(j * (2 * SEG) + SEG, SEG), :]
            spans = [(4 * (place.half * HALF + j), 0, SEG)]
            for m in range(LISTED):
                spans.append((entries[0, n * SLOT + m], SEG + m * BLOCK, BLOCK))

            def keyed(src, size):
                return kv[pl.ds(src, 2)].reshape(SEG, HD) if size == SEG else kv[src]

            top8 = None
            for src, at, size in spans:
                k = keyed(src, size)
                s = lax.dot_general(k, q, NT, preferred_element_type=F32)
                e_ref[at:at + size, :] = s
                high = fold(s, jnp.max)
                top8 = high if top8 is None else jnp.maximum(top8, high)
            factor = SCALE * LOG2E
            top = jnp.maximum(jnp.max(top8, axis=0, keepdims=True) * factor, sink2)
            sum8 = jnp.zeros((8, SEG), F32)
            dot8 = jnp.zeros((8, SEG), F32)
            for src, at, size in spans:
                v = keyed(src + 2, size)
                dp = lax.dot_general(v, g, NT, preferred_element_type=F32)
                e = jnp.exp2(e_ref[at:at + size, :] * factor - top)
                e_ref[at:at + size, :] = e
                p_ref[at:at + size, :] = dp
                sum8 = sum8 + fold(e, jnp.sum)
                dot8 = dot8 + fold(e * dp, jnp.sum)
            sink_e = jnp.exp2(sink2 - top)
            total = sink_e + jnp.sum(sum8, axis=0, keepdims=True)
            inv = 1.0 / total
            delta = jnp.sum(dot8, axis=0, keepdims=True) * inv
            sink_sum[...] = sink_sum[...] - sink_e * inv * delta
            dq_t = jnp.zeros((HD, SEG), F32)
            for m, (src, at, size) in enumerate(spans):
                w = e_ref[at:at + size, :] * inv
                ds = (w * (p_ref[at:at + size, :] - delta)).astype(BF16)
                w = w.astype(BF16)
                tv = jnp.dot(w, g, preferred_element_type=F32)
                tk = jnp.dot(ds, q, preferred_element_type=F32)
                if m == 0:
                    own_k[rows_of(n * SEG, SEG), :] = tk
                    own_v[rows_of(n * SEG, SEG), :] = tv
                else:
                    slot = n * SLOT + m - 1
                    before = entries[1, slot]
                    term_k[slot] = tk + term_k[before]
                    term_v[slot] = tv + term_v[before]
                k = keyed(src, size)
                dq_t = dq_t + lax.dot_general(k, ds, TN, preferred_element_type=F32)
            rows = rows_of(n * SEG, SEG)
            dq[rows, :] = (dq_t * SCALE).T.astype(BF16)
            by_relay, relay = place.relayed(j)
            slot = (head_of - place.row_head) * 4 + div(j, 4)

            @pl.when(by_relay)
            def _():
                to = relay_dq.at[rows_of(slot * SEG, SEG)]
                remote(dq.at[rows], to, dq_send, relay_dq_recv.at[slot], relay).start()

            @pl.when(jnp.logical_not(by_relay))
            def _():
                remote(dq.at[rows], gq.at[0, :, cols], dq_send, out_recv.at[0], place.owner(j)).start()

        step = HALF // CHUNKS
        for c in range(CHUNKS):
            @pl.loop(0, step)
            def _(i):
                n = c * step + i
                j = taken(head_of, n)
                for b in range(2):
                    last = entries[2, 2 * segment(place.core, j) + b]
                    at = n * (2 * SEG) + b * BLOCK
                    far[rows_of(at, BLOCK), :] = (term_k[last] * SCALE).astype(BF16)
                    far[rows_of(at + SEG, BLOCK), :] = term_v[last].astype(BF16)

            part = pl.ds(c * step * 2 * SEG, step * 2 * SEG)
            remote(far.at[part], near.at[part], far_send.at[c], far_recv.at[c], place.sibling).start()

        mine_a = sink_a.at[2 * place.pair_core + place.core]
        mine_a[...] = jnp.broadcast_to(jnp.sum(sink_sum[...], axis=1, keepdims=True), (1, BLOCK))
        for t, peer in enumerate((place.sibling, *place.twins)):
            remote(mine_a, mine_a, a_send, a_recv, peer).start()

        def collect(c):
            part = pl.ds(c * step * 2 * SEG, step * 2 * SEG)
            remote(far.at[part], near.at[part], far_send.at[c], far_recv.at[c], place.sibling).wait()

            @pl.loop(0, step)
            def _(i):
                n = c * step + i
                j = taken(head_of, n)
                for b in range(2):
                    last = entries[2, 2 * segment(place.half, j) + b]
                    at = n * (2 * SEG) + b * BLOCK
                    own = rows_of(n * SEG + b * BLOCK, BLOCK)
                    tk = (own_k[own, :] + term_k[last]) * SCALE + near[rows_of(at, BLOCK), :].astype(F32)
                    tv = own_v[own, :] + term_v[last] + near[rows_of(at + SEG, BLOCK), :].astype(F32)
                    fin[rows_of(at, BLOCK), :] = tk.astype(BF16)
                    fin[rows_of(at + SEG, BLOCK), :] = tv.astype(BF16)
                at = n * (2 * SEG)
                to = place.owner(j)
                by_relay, relay = place.relayed(j)
                slot = (head_of - place.row_head) * 4 + div(j, 4)

                @pl.when(by_relay)
                def _():
                    both = relay_kv.at[rows_of(slot * (2 * SEG), 2 * SEG)]
                    remote(fin.at[rows_of(at, 2 * SEG)], both, fin_send, relay_kv_recv.at[slot], relay).start()

                @pl.when(jnp.logical_not(by_relay))
                def _():
                    remote(fin.at[rows_of(at, SEG)], gk.at[0, :, cols], fin_send, out_recv.at[1], to).start()
                    remote(fin.at[rows_of(at + SEG, SEG)], gv.at[0, :, cols], fin_send, out_recv.at[2], to).start()

        collect(0)
        three = sink_a.at[pl.ds(0, 3)]
        remote(three, three, a_send, a_recv, place.sibling).wait()
        plane = div(place.plane, 2)
        mine_b = sink_b.at[plane]
        mine_b[...] = (sink_a[0] + sink_a[1]) + (sink_a[2] + sink_a[3])

        @pl.loop(1, PLANES)
        def _(i):
            remote(mine_b, mine_b, b_send, b_recv, place.other_plane(i)).start()

        collect(1)
        collect(2)
        seven = sink_b.at[pl.ds(0, PLANES - 1)]
        remote(seven, seven, b_send, b_recv, place.sibling).wait()
        total = sink_b[0]
        for i in range(1, PLANES):
            total = total + sink_b[i]
        sink_c[...] = total

        @pl.loop(0, HALF)
        def _(j):
            remote(sink_c, sink_out.at[head_of], c_send, c_recv, place.owner(j)).start()

        collect(3)
        remote(fin, fin, fin_send, out_recv.at[0], place.sibling).wait_send()
        remote(dq, dq, dq_send, out_recv.at[0], place.sibling).wait_send()

        @pl.loop(0, HALF)
        def _(j):
            remote(sink_c, sink_out.at[head_of], c_send, c_recv, place.owner(j)).wait_send()

    @pl.when(jnp.logical_not(place.is_home))
    def _():
        def each(work):
            @pl.loop(0, 4)
            def _(t):
                @pl.loop(0, place.homes)
                def _(i):
                    head, _ = place.row_home(i)
                    first = div(8 * head, 5) + HALF
                    j = rem(first - rem(first - place.x, 4) + HALF - 4 * div(t, 2) - 8 * rem(t, 2), HALF)

                    s = segment(place.half, j)

                    @pl.when(div(s, 4) != place.y)
                    def _():
                        work(i * 4 + div(j, 4), columns(head), (place.plane + place.row_core, s))

        def pass_dq(slot, cols, to):
            part = relay_dq.at[rows_of(slot * SEG, SEG)]
            remote(part, part, relay_send, relay_dq_recv.at[slot], place.sibling).wait_recv()
            remote(part, gq.at[0, :, cols], relay_send, out_recv.at[0], to).start()

        def pass_kv(slot, cols, to):
            at = slot * (2 * SEG)
            both = relay_kv.at[rows_of(at, 2 * SEG)]
            remote(both, both, relay_send, relay_kv_recv.at[slot], place.sibling).wait_recv()
            remote(relay_kv.at[rows_of(at, SEG)], gk.at[0, :, cols], relay_send, out_recv.at[1], to).start()
            remote(relay_kv.at[rows_of(at + SEG, SEG)], gv.at[0, :, cols], relay_send, out_recv.at[2], to).start()

        each(pass_dq)
        each(pass_kv)

        @pl.loop(0, 3 * place.homes * (4 - place.inside))
        def _(i):
            part = relay_dq.at[pl.ds(0, SEG)]
            remote(part, part, relay_send, relay_dq_recv.at[0], place.sibling).wait_send()

    remote(lists_in, lists_in, list_send, list_recv, place.sibling).wait_send()
    for t, ref in enumerate((q_in, g_in)):
        remote(ref, ref, qg_send.at[t], qg_recv.at[0], place.sibling).wait_send()
    for t, ref in enumerate((gq, gk, gv)):
        remote(ref, ref, dq_send, out_recv.at[t], place.sibling).wait_recv()
    remote(sink_out, sink_out, c_send, c_recv, place.sibling).wait_recv()


def settle_kernel(gq, gk, gv, out_q, out_k, out_v):
    out_q[...] = gq[...]
    out_k[...] = gk[...]
    out_v[...] = gv[...]


def body(query_in, key_in, value_in, grad_out, key_blocks, sink_logits):
    any_spec = pl.BlockSpec(memory_space=pl.ANY)
    smem_spec = pl.BlockSpec(memory_space=pltpu.SMEM)
    dma = pltpu.SemaphoreType.DMA
    shape = jax.ShapeDtypeStruct
    vmem = pltpu.VMEM
    local = local_of(lax.axis_index("ctx"))
    turns = turn(jnp.arange(HEADS, dtype=jnp.int32), local)
    lane = jnp.arange(BLOCK, dtype=jnp.int32)
    tiled = jnp.tile(jnp.pad(key_blocks[:, 0, :] + 1, ((0, 0), (0, SLOT - LISTED))), (1, HALF))
    lists = jnp.where(div(lane, SLOT)[None, :] == turns[:, None], tiled, 0)[:, None, :]
    tok = query_in.shape
    halves = (2, BLOCK, tok[2])
    gq, gk, gv, sink_rows = pl.pallas_call(
        fused_kernel,
        out_shape=(shape(tok, BF16), shape(tok, BF16), shape(tok, BF16), shape((HEADS, 1, BLOCK), F32)),
        in_specs=[any_spec] * 5 + [smem_spec],
        out_specs=(any_spec,) * 4,
        scratch_shapes=[
            vmem((NSEG * 4, BLOCK, HD), BF16),
            vmem((HALF * 2 * SEG, HD), BF16),
            vmem((HALF, 1, BLOCK), jnp.int32),
            vmem((8, BLOCK), jnp.int32),
            pltpu.SMEM((8, BLOCK), jnp.int32),
            vmem((HALF * SEG, HD), BF16),
            vmem((HALF * SLOT, BLOCK, HD), F32),
            vmem((HALF * SLOT, BLOCK, HD), F32),
            vmem((HALF * SEG, HD), F32),
            vmem((HALF * SEG, HD), F32),
            vmem((HALF * 2 * SEG, HD), BF16),
            vmem((HALF * 2 * SEG, HD), BF16),
            vmem((HALF * 2 * SEG, HD), BF16),
            vmem((KEYS, SEG), F32),
            vmem((KEYS, SEG), F32),
            vmem((1, SEG), F32),
            vmem((4, 1, BLOCK), F32),
            vmem((PLANES, 1, BLOCK), F32),
            vmem((1, BLOCK), F32),
            dma, dma, dma((2,)), dma((HALF,)), dma, dma, dma((2,)), dma((HALF,)), dma, dma,
            vmem((3 * 4 * SEG, HD), BF16), vmem((3 * 4 * 2 * SEG, HD), BF16),
            dma((12,)), dma((12,)), dma,
            dma((3,)), dma((CHUNKS,)), dma((CHUNKS,)), dma, dma, dma, dma, dma, dma, dma,
        ],
        compiler_params=pltpu.CompilerParams(
            collective_id=0, has_side_effects=True, vmem_limit_bytes=56 * 2**20
        ),
        name="fused",
    )(query_in, key_in.reshape(halves), value_in.reshape(halves), grad_out, lists, sink_logits)
    out = pl.pallas_call(
        settle_kernel,
        out_shape=(shape(tok, BF16),) * 3,
        in_specs=[pl.BlockSpec(memory_space=vmem)] * 3,
        out_specs=(pl.BlockSpec(memory_space=vmem),) * 3,
        name="settle",
    )(gq, gk, gv)
    return (*out, sink_rows[:, 0, 0])


def solution(mesh):
    placed = (
        P("dp", "ctx", None),
        P("dp", "ctx", None),
        P("dp", "ctx", None),
        P("dp", "ctx", None),
        P(None, "ctx", None),
        P(),
    )
    return jax.shard_map(
        body,
        mesh=mesh,
        in_specs=placed,
        out_specs=(P("dp", "ctx", None), P("dp", "ctx", None), P("dp", "ctx", None), P()),
        check_vma=False,
    )
```

time: 292 us -> 144 us (0.49)
  the two profiles are of different devices: /device:TPU:1 before, /device:TPU:122 now
where the time goes in v2:
time: 144 us
  Pallas kernels  140 us (97%)
  local copies, waits for them, and re-layouts  2.25 us (2%)
    pallas_call x1, Pallas kernels, body(): pl.pallas_call(fused_kernel, out_shape=(shape(tok, BF16), shape(tok, BF16...  137 us

profile of v2, /device:TPU:122, one launch (start us, length us, event | category | flops | bytes accessed | tf_op | source)
XLA Modules:
  0.0 143.8 jit_solution(886173473910158674)
XLA Ops:
  0.7 0.0 copy-start.1
  0.7 0.7 copy-done.1
  1.3 0.1 copy.15
  1.5 0.1 tile.11
  1.6 0.7 compare_select_fusion.lists_in
  2.2 137.4 %fused.1 = (bf16[1,256,1280]{2,1,0:T(8,128)(2,1)}, bf16[1,256,1280]{2,1,0:T(8,128)(2,1)}, bf16[1,256,1280]{2,1,0:T(8,128)(2,1)}, f32[10,1,128]{2,1,0:T(1,128)}) custom-call(bf16[1,256,1280]{2,1,0:T(8,128)(2,1)} %q_in.1, bf16[2,128,1280]{2,1,0:T(8,128)(2,1)} %bitcast.4, bf16[2,128,1280]{2,1,0:T(8,128)(2,1)} %bitcast.5, bf16[1,256,1280]{2,1,0:T(8,128)(2,1)} %g_in.1, ...), custom_call_target="tpu_custom_call" | custom-call | tf_op jit(solution)/shard_map/fused/pallas_call | solution.py:512
  139.6 2.8 %settle.1 = (bf16[1,256,1280]{2,1,0:T(8,128)(2,1)}, bf16[1,256,1280]{2,1,0:T(8,128)(2,1)}, bf16[1,256,1280]{2,1,0:T(8,128)(2,1)}) custom-call(bf16[1,256,1280]{2,1,0:T(8,128)(2,1)} %get-tuple-element.11.gq, bf16[1,256,1280]{2,1,0:T(8,128)(2,1)} %get-tuple-element.12.gk, bf16[1,256,1280]{2,1,0:T(8,128)(2,1)} %get-tuple-element.13.gv), custom_call_target="tpu_custom_call" | custom-call | tf_op jit(solution)/shard_map/settle/pallas_call | solution.py:547
  142.4 0.0 copy-start
  142.4 0.7 copy-done
  143.1 0.7 slice_reduce_fusion
  (5 shorter events, 0.0 us)
Async XLA Ops:
  0.7 0.7 copy-start.1
  142.4 0.7 copy-start

commit v3 on v2

--- a/solution.py
+++ b/solution.py
@@ -18,7 +18,9 @@
 SLOT = 8
 EMPTY = 6
 CHUNKS = 4
-EARLY = 10
+EARLY = 0
+PIECES = 4
+PIECE = SEG // PIECES
 PLANES = 8
 LOG2E = math.log2(math.e)
 SCALE = 1.0 / math.sqrt(HD)
@@ -122,7 +124,8 @@
     def relayed(self, j):
         x = rem(j, 4)
         device = (self.plane + self.core, 4 * self.y + x)
-        return is_spare(self.y, x) & (div(segment(self.half, j), 4) != self.y), device
+        outer = (self.odd == 1) | (self.pair_head != self.row_head + 1)
+        return is_spare(self.y, x) & (div(segment(self.half, j), 4) != self.y) & outer, device
 
     def other_plane(self, i):
         return (rem(self.plane + self.core + 2 * i, 2 * PLANES), self.ctx)
@@ -240,15 +243,19 @@
         target = place.home(head)
         remote(lists_in.at[head], lists.at[place.local], list_send, list_recv, target).start()
 
-    @pl.loop(0, HEADS)
-    def _(i):
-        head = place.sent_to(i)
-        cols = columns(head)
-        target = place.home(head)
-        at = 4 * ((1 - place.target_core) * HALF + place.local)
-        sem = kv_recv.at[place.local]
-        remote(k_in.at[:, :, cols], kv.at[pl.ds(at, 2)], kv_send.at[0], sem, target).start()
-        remote(v_in.at[:, :, cols], kv.at[pl.ds(at + 2, 2)], kv_send.at[1], sem, target).start()
+    for block in range(2):
+        for p in range(PIECES // 2):
+            rows = pl.ds(p * PIECE, PIECE)
+
+            @pl.loop(0, HEADS)
+            def _(i):
+                head = place.sent_to(i)
+                cols = columns(head)
+                target = place.home(head)
+                at = 4 * ((1 - place.target_core) * HALF + place.local) + block
+                sem = kv_recv.at[place.local]
+                remote(k_in.at[block, rows, cols], kv.at[at, rows], kv_send.at[0], sem, target).start()
+                remote(v_in.at[block, rows, cols], kv.at[at + 2, rows], kv_send.at[1], sem, target).start()
 
     def pass_on(start, stop):
         @pl.loop(start, stop)
@@ -405,8 +412,10 @@
 
                 @pl.when(by_relay)
                 def _():
-                    both = relay_kv.at[rows_of(slot * (2 * SEG), 2 * SEG)]
-                    remote(fin.at[rows_of(at, 2 * SEG)], both, fin_send, relay_kv_recv.at[slot], relay).start()
+                    for t in range(2):
+                        to = relay_kv.at[rows_of(slot * (2 * SEG) + t * SEG, SEG)]
+                        sem = relay_kv_recv.at[2 * slot + t]
+                        remote(fin.at[rows_of(at + t * SEG, SEG)], to, fin_send, sem, relay).start()
 
                 @pl.when(jnp.logical_not(by_relay))
                 def _():
@@ -458,7 +467,7 @@
 
                     s = segment(place.half, j)
 
-                    @pl.when(div(s, 4) != place.y)
+                    @pl.when((div(s, 4) != place.y) & ((place.odd == 1) | (i != 1)))
                     def _():
                         work(i * 4 + div(j, 4), columns(head), (place.plane + place.row_core, s))
 
@@ -468,16 +477,15 @@
             remote(part, gq.at[0, :, cols], relay_send, out_recv.at[0], to).start()
 
         def pass_kv(slot, cols, to):
-            at = slot * (2 * SEG)
-            both = relay_kv.at[rows_of(at, 2 * SEG)]
-            remote(both, both, relay_send, relay_kv_recv.at[slot], place.sibling).wait_recv()
-            remote(relay_kv.at[rows_of(at, SEG)], gk.at[0, :, cols], relay_send, out_recv.at[1], to).start()
-            remote(relay_kv.at[rows_of(at + SEG, SEG)], gv.at[0, :, cols], relay_send, out_recv.at[2], to).start()
+            for t, ref in enumerate((gk, gv)):
+                part = relay_kv.at[rows_of(slot * (2 * SEG) + t * SEG, SEG)]
+                remote(part, part, relay_send, relay_kv_recv.at[2 * slot + t], place.sibling).wait_recv()
+                remote(part, ref.at[0, :, cols], relay_send, out_recv.at[1 + t], to).start()
 
         each(pass_dq)
         each(pass_kv)
 
-        @pl.loop(0, 3 * place.homes * (4 - place.inside))
+        @pl.loop(0, 3 * 2 * (4 - place.inside))
         def _(i):
             part = relay_dq.at[pl.ds(0, SEG)]
             remote(part, part, relay_send, relay_dq_recv.at[0], place.sibling).wait_send()
@@ -490,7 +498,9 @@
     remote(sink_out, sink_out, c_send, c_recv, place.sibling).wait_recv()
 
 
-def settle_kernel(gq, gk, gv, out_q, out_k, out_v):
+def settle_kernel(gq, gk, gv, sink_rows, out_q, out_k, out_v, out_sink):
+    for head in range(HEADS):
+        out_sink[head] = sink_rows[head, 0, 0]
     out_q[...] = gq[...]
     out_k[...] = gk[...]
     out_v[...] = gv[...]
@@ -536,7 +546,7 @@
             vmem((1, BLOCK), F32),
             dma, dma, dma((2,)), dma((HALF,)), dma, dma, dma((2,)), dma((HALF,)), dma, dma,
             vmem((3 * 4 * SEG, HD), BF16), vmem((3 * 4 * 2 * SEG, HD), BF16),
-            dma((12,)), dma((12,)), dma,
+            dma((12,)), dma((24,)), dma,
             dma((3,)), dma((CHUNKS,)), dma((CHUNKS,)), dma, dma, dma, dma, dma, dma, dma,
         ],
         compiler_params=pltpu.CompilerParams(
@@ -546,12 +556,12 @@
     )(query_in, key_in.reshape(halves), value_in.reshape(halves), grad_out, lists, sink_logits)
     out = pl.pallas_call(
         settle_kernel,
-        out_shape=(shape(tok, BF16),) * 3,
-        in_specs=[pl.BlockSpec(memory_space=vmem)] * 3,
-        out_specs=(pl.BlockSpec(memory_space=vmem),) * 3,
+        out_shape=(shape(tok, BF16), shape(tok, BF16), shape(tok, BF16), shape((HEADS,), F32)),
+        in_specs=[pl.BlockSpec(memory_space=vmem)] * 3 + [smem_spec],
+        out_specs=(*(pl.BlockSpec(memory_space=vmem),) * 3, smem_spec),
         name="settle",
-    )(gq, gk, gv)
-    return (*out, sink_rows[:, 0, 0])
+    )(gq, gk, gv, sink_rows)
+    return out
 
 
 def solution(mesh):

time: 144 us -> 139 us (0.965)
  the two profiles are of different devices: /device:TPU:122 before, /device:TPU:145 now
where the time goes in v3:
time: 139 us
  Pallas kernels  137 us (99%)
    pallas_call x1, Pallas kernels, body(): pl.pallas_call(fused_kernel, out_shape=(shape(tok, BF16), shape(tok, BF16...  134 us
    pallas_call x1, Pallas kernels, body(): pl.pallas_call(settle_kernel, out_shape=(shape(tok, BF16), shape(tok, BF1...  2.81 us

profile of v3, /device:TPU:145, one launch (start us, length us, event | category | flops | bytes accessed | tf_op | source)
XLA Modules:
  0.0 139.2 jit_solution(3853692754761890007)
XLA Ops:
  0.7 0.0 copy-start
  0.7 0.7 copy-done
  1.3 0.1 copy.15
  1.5 0.1 tile.11
  1.6 0.7 compare_select_fusion.lists_in
  2.2 134.1 %fused.1 = (bf16[1,256,1280]{2,1,0:T(8,128)(2,1)}, bf16[1,256,1280]{2,1,0:T(8,128)(2,1)}, bf16[1,256,1280]{2,1,0:T(8,128)(2,1)}, f32[10,1,128]{2,1,0:T(1,128)}) custom-call(bf16[1,256,1280]{2,1,0:T(8,128)(2,1)} %q_in.1, bf16[2,128,1280]{2,1,0:T(8,128)(2,1)} %bitcast.4, bf16[2,128,1280]{2,1,0:T(8,128)(2,1)} %bitcast.5, bf16[1,256,1280]{2,1,0:T(8,128)(2,1)} %g_in.1, ...), custom_call_target="tpu_custom_call" | custom-call | tf_op jit(solution)/shard_map/fused/pallas_call | solution.py:522
  136.3 2.8 %settle.1 = (bf16[1,256,1280]{2,1,0:T(8,128)(2,1)}, bf16[1,256,1280]{2,1,0:T(8,128)(2,1)}, bf16[1,256,1280]{2,1,0:T(8,128)(2,1)}, f32[10]{0:T(128)}) custom-call(bf16[1,256,1280]{2,1,0:T(8,128)(2,1)} %get-tuple-element.8.gq, bf16[1,256,1280]{2,1,0:T(8,128)(2,1)} %get-tuple-element.9.gk, bf16[1,256,1280]{2,1,0:T(8,128)(2,1)} %get-tuple-element.10.gv, ...), custom_call_target="tpu_custom_call" | custom-call | tf_op jit(solution)/shard_map/settle/pallas_call | solution.py:557
  (5 shorter events, 0.0 us)
Async XLA Ops:
  0.7 0.7 copy-start
